TPU v7x, 512 devices: a whole 4x8x8 slice. The times are simulated.
512 devices in a mesh: req: 32 (over z, y_lo), tp: 16 (over y_hi, x, core).
Axes of the slice: x: 4, y: 8 (y_hi: 2, y_lo: 4; y = y_hi * 4 + y_lo), z: 8, core: 2. Of those that a mesh axis runs over, the one named last changes fastest.
Arguments:
- tokens: bfloat16 [16384, 4096], P(('req', 'tp')), parts along dimension 0, may hold values from -400 to 400
- norm_gain: bfloat16 [4096], replicated, may hold values from 0.099609375 to 1.8984375
- qkv_weight: bfloat16 [4096, 6144], P(None, 'tp'), may hold values from -0.46875 to 0.46875
- out_weight: bfloat16 [2048, 4096], P('tp'), may hold values from -0.5 to 0.5
- segment_ids: int32 [16384], P('req'), parts along dimension 0, may hold values from 0 to 7, never falling along the last dimension, each value on 1 to 170 neighbouring positions
- prefix_pages: int32 [256], P('req'), parts along dimension 0, may hold values from 1 to 16, 48 in all
- page_order: int32 [1536], P('req'), parts along dimension 0, may hold values from 0 to 47, each once
- fresh_order: int32 [1280], P('req'), parts along dimension 0, may hold values from 0 to 39, each once
- cache_pool: bfloat16 [2, 16, 1536, 16, 128], P(None, 'tp', 'req'), parts along dimension 2, may hold values from -6 to 6
Outputs:
- attn_out: bfloat16 [16384, 4096], P(('req', 'tp')), parts along dimension 0
- fresh_pages: bfloat16 [2, 16, 1280, 16, 128], P(None, 'tp', 'req'), parts along dimension 2
There are 32 independent parts, one for each index of `req`. A program takes and returns all parts, laid end to end along the dimension named above; an argument that names none is the same for every part. Nothing has to cross between parts.
Inputs may be any that keep to these rules, and one draw needn't show every extreme that they name: `segment_ids`: segment numbers never fall; every prompt has at least one new token and one has exactly 170. `prefix_pages`: they sum to 48; the largest is 16. `page_order`: every page once. `fresh_order`: every page once.
All inputs are finite; a program needn't handle non-finite values.
Results may differ from a plain program's by a relative error of at most 0.014.
Values may be sent and summed in bfloat16 or wider, within the bound.
No kernel may reach another device: no remote copies, remote signals or barrier semaphores. Data moves between devices by JAX's collectives and lax.ppermute only.
A program may use at most 64 MiB of HBM per device.

v0:
```python
import jax
import jax.numpy as jnp
from jax import lax
from jax.sharding import PartitionSpec as P

MODEL_HEADS = 32


def layer_norm(values, gain):
    values = values.astype(jnp.float32)
    center = values - jnp.mean(values, axis=-1, keepdims=True)
    spread = jnp.mean(center * center, axis=-1, keepdims=True)
    return (center * lax.rsqrt(spread + 1e-05) * gain.astype(jnp.float32)).astype(jnp.bfloat16)


def token_layout(segment_ids, prefix_pages, page_order, fresh_order, page_len):
    seq_count = prefix_pages.shape[0]
    tok_count = segment_ids.shape[0]
    labels = jnp.arange(seq_count, dtype=jnp.int32)
    member = (segment_ids[:, None] == labels[None, :]).astype(jnp.int32)
    counts = jnp.sum(member, axis=0)
    starts = jnp.cumsum(counts) - counts
    token_index = jnp.arange(tok_count, dtype=jnp.int32)
    in_prompt = token_index - jnp.sum(member * starts[None, :], axis=1)
    prefix_len = prefix_pages * page_len
    position = in_prompt + jnp.sum(member * prefix_len[None, :], axis=1)
    fresh_counts = (counts + page_len - 1) // page_len
    fresh_starts = jnp.cumsum(fresh_counts) - fresh_counts
    page_slot = jnp.sum(member * fresh_starts[None, :], axis=1) + in_prompt // page_len
    target = jnp.take(fresh_order, page_slot) * page_len + in_prompt % page_len
    page_count = page_order.shape[0]
    cache_starts = jnp.cumsum(prefix_pages) - prefix_pages
    logical = (
        jnp.zeros((page_count,), jnp.int32)
        .at[page_order]
        .set(jnp.arange(page_count, dtype=jnp.int32))
    )
    holder = jnp.sum((logical[:, None] >= cache_starts[None, :]).astype(jnp.int32), axis=1) - 1
    holder_start = jnp.sum(
        (holder[:, None] == labels[None, :]).astype(jnp.int32) * cache_starts[None, :], axis=1
    )
    slot_index = jnp.arange(page_len, dtype=jnp.int32)
    key_owner = jnp.repeat(holder, page_len)
    key_pos = ((logical - holder_start)[:, None] * page_len + slot_index[None, :]).reshape(-1)
    return (in_prompt, position, target, key_owner, key_pos)


def attention_mask(segment_ids, in_prompt, position, key_owner, key_pos):
    cache_ok = segment_ids[:, None] == key_owner[None, :]
    new_ok = (segment_ids[:, None] == segment_ids[None, :]) & (
        in_prompt[None, :] <= in_prompt[:, None]
    )
    allowed = jnp.concatenate([cache_ok, new_ok], axis=1)
    key_all = jnp.concatenate([key_pos, position])
    distance = (position[:, None] - key_all[None, :]).astype(jnp.float32)
    return (allowed, distance)


def attend_head(queries, key_rows, values, alibi_slope, allowed, distance):
    scores = lax.dot_general(
        queries, key_rows, (((1,), (1,)), ((), ())), preferred_element_type=jnp.float32
    )
    scores = scores * queries.shape[1] ** (-0.5) - alibi_slope * distance
    scores = jnp.where(allowed, scores, -1e30)
    peak_score = jnp.max(scores, axis=1, keepdims=True)
    weights = jnp.exp(scores - peak_score)
    weights_bf = (weights / jnp.sum(weights, axis=1, keepdims=True)).astype(jnp.bfloat16)
    return jnp.dot(weights_bf, values, preferred_element_type=jnp.float32).astype(jnp.bfloat16)


def body(
    tokens,
    norm_gain,
    qkv_weight,
    out_weight,
    segment_ids,
    prefix_pages,
    page_order,
    fresh_order,
    cache_pool,
):
    head_dev = cache_pool.shape[1]
    page_len = cache_pool.shape[3]
    head_size = cache_pool.shape[4]
    tp_size = lax.axis_size("tp")
    first_head = lax.axis_index("tp") * head_dev
    normed = layer_norm(tokens, norm_gain)
    projected = jnp.dot(
        lax.all_gather(normed, "tp", axis=0, tiled=True),
        qkv_weight,
        preferred_element_type=jnp.float32,
    ).astype(jnp.bfloat16)
    tok_count = projected.shape[0]
    in_prompt, position, target, key_owner, key_pos = token_layout(
        segment_ids, prefix_pages, page_order, fresh_order, page_len
    )
    allowed, distance = attention_mask(segment_ids, in_prompt, position, key_owner, key_pos)
    per_head = projected.reshape(tok_count, head_dev, 3, head_size)
    step_heads = MODEL_HEADS // (head_dev * tp_size)
    alibi_slope = jnp.exp2(
        -8.0 * (first_head + 0 + 1).astype(jnp.float32) * step_heads / MODEL_HEADS
    )
    key_rows = jnp.concatenate([cache_pool[0, 0].reshape(-1, head_size), per_head[:, 0, 1]], axis=0)
    values = jnp.concatenate([cache_pool[1, 0].reshape(-1, head_size), per_head[:, 0, 2]], axis=0)
    contexts = attend_head(per_head[:, 0, 0], key_rows, values, alibi_slope, allowed, distance)
    summed = lax.psum_scatter(
        jnp.dot(contexts, out_weight, preferred_element_type=jnp.float32).astype(jnp.bfloat16),
        "tp",
        scatter_dimension=0,
        tiled=True,
    )
    fresh_total = fresh_order.shape[0]
    new_kv = per_head[:, :, 1:3].transpose(2, 1, 0, 3)
    fresh_pages = (
        jnp.zeros((2, head_dev, fresh_total * page_len, head_size), jnp.bfloat16)
        .at[:, :, target]
        .set(new_kv)
    )
    return (summed, fresh_pages.reshape(2, head_dev, fresh_total, page_len, head_size))


def solution(mesh):
    placed = (
        P(("req", "tp"), None),
        P(),
        P(None, "tp"),
        P("tp", None),
        P("req"),
        P("req"),
        P("req"),
        P("req"),
        P(None, "tp", "req", None, None),
    )
    return jax.shard_map(
        body,
        mesh=mesh,
        in_specs=placed,
        out_specs=(P(("req", "tp"), None), P(None, "tp", "req", None, None)),
        check_vma=False,
    )
```

profile of v0, /device:TPU:8, one launch (start us, length us, event | category | flops | bytes accessed | tf_op | source)
XLA Modules:
  0.0 233.2 jit_solution(15736835718099933660)
XLA Ops:
  7.2 0.0 copy-start
  7.2 0.0 all-gather.2.cloned.1.call-start
  7.2 1.2 convert_reduce_fusion
  8.5 1.2 fusion.7
  9.7 0.7 convert_element_type.37
  10.4 1.8 fusion.9
  12.2 0.0 all-gather.2.cloned.1.call-update
  12.2 0.0 reduce-scatter.2.cloned.1.call-start
  12.3 0.8 convert_reduce_fusion.1
  13.1 0.2 reduce-window.26
  13.3 0.2 reduce-window.27
  13.5 0.8 reduce-window.25
  14.3 0.7 compare_select_fusion.11
  15.0 0.7 scatter_custom_fusion
  15.7 0.7 bitcast_subtract_fusion.1
  16.4 0.1 convert_reduce_fusion.2
  16.5 0.1 select_reduce_fusion.3
  16.6 0.1 iota_add_fusion
  16.6 0.1 add.182
  16.7 0.1 broadcast_in_dim.16
  16.8 0.1 eq.29
  16.9 0.8 select_reduce_fusion
  17.7 1.7 compare_and_fusion
  19.4 1.7 broadcast_compare_fusion
  21.1 1.8 fusion.26
  22.9 75.8 %all-gather.2.cloned.1.call-done = bf16[512,4096]{1,0:T(8,128)(2,1)} async-done(((bf16[32,4096]{1,0:T(8,128)(2,1)}), bf16[512,4096]{1,0:T(8,128)(2,1)}) %all-gather.2.cloned.1.call-update) | async-done | bytes 4194320 | tf_op jit(solution)/shard_map/all_gather | solution.py:89
  98.8 4.0 %convolution_convert_fusion.1 = bf16[512,384]{0,1:T(8,128)(2,1)S(1)} fusion(bf16[512,4096]{1,0:T(8,128)(2,1)} %all-gather.2.cloned.1.call-done, bf16[4096,384]{1,0:T(8,128)(2,1)S(1)} %copy-done), kind=kOutput, calls=%fused_computation.10 | convolution fusion | flops 1610809344 | bytes 7733248 | tf_op jit(solution)/shard_map/dot_general | solution.py:88
  102.8 0.8 slice_bitcast_fusion
  103.6 1.7 copy.20
  105.3 1.7 copy.19
  106.9 2.3 %fusion.30 = (f32[512]{0:T(512)S(1)}, f32[512,1280]{1,0:T(8,128)S(1)}) fusion(s32[1280]{0:T(1024)S(1)} %pad_add_fusion, s32[512]{0:T(512)} %copy-done.6, f32[]{:T(128)S(6)} %exp2.7, bf16[512,128]{1,0:T(8,128)(2,1)} %copy.19, bf16[768,128]{1,0:T(8,128)(2,1)} %bitcast.83, bf16[512,1,3,128]{0,3,2,1:T(8,128)(2,1)S(1)} %bitcast.80, ...), kind=kOutput, calls=%fused_computation.117 | convolution fusion | flops 173669888 | bytes 3747844 | tf_op jit(solution)/shard_map/dot_general | solution.py:60
  109.3 1.5 copy-done.1
  110.8 0.5 fusion.2
  111.3 6.3 %convolution_convert_fusion = bf16[512,4096]{1,0:T(8,128)(2,1)} fusion(bf16[128,4096]{1,0:T(8,128)(2,1)} %param.12, f32[512,1280]{1,0:T(8,128)} %copy-done.1, f32[512]{0:T(512)S(1)} %fusion.2, f32[512]{0:T(512)} %copy-done.7, bf16[512,128]{1,0:T(8,128)(2,1)S(1)} %copy-done.5, bf16[768,128]{1,0:T(8,128)(2,1)S(1)} %bitcast.82), kind=kOutput, calls=%fused_computation.2 | convolution fusion | flops 709427200 | bytes 8196096 | tf_op jit(solution)/shard_map/dot_general | solution.py:107
  117.7 0.0 reduce-scatter.2.cloned.1.call-update
  117.7 0.6 copy-done.2
  118.3 0.6 fusion.29
  119.0 0.7 fusion.27
  119.7 0.7 fusion.28
  120.4 4.5 %compare_select_fusion.2 = (s32[512,1]{0,1:T(1,128)S(1)}, s32[512,1]{0,1:T(1,128)S(1)}) fusion(s32[]{:T(128)} %bitcast.46, s32[]{:T(128)} %bitcast.47, s32[]{:T(128)} %bitcast.48, s32[]{:T(128)} %bitcast.49, s32[]{:T(128)} %bitcast.50, s32[]{:T(128)} %bitcast.52, s32[]{:T(128)} %bitcast.51, s32[512,1]{0,1:T(1,128)S(1)} %bitcast.87, s32[512,1]{0,1:T(1,128)S(1)} %bitcast.84), kind=kLoop, calls=%fused_computation.72 | loop fusion | flops 16384 | bytes 8220 | tf_op jit(solution)/shard_map/jit(_take)/gather | solution.py:30
  124.9 0.2 compare_reduce_fusion.32
  125.1 20.5 %select_select_fusion = s32[512]{0:T(512)S(1)} fusion(pred[512]{0:T(512)(128)(4,1)S(1)} %get-tuple-element.39, pred[512]{0:T(512)(128)(4,1)S(1)} %get-tuple-element.38, pred[512]{0:T(512)(128)(4,1)S(1)} %get-tuple-element.40, pred[512]{0:T(512)(128)(4,1)S(1)} %get-tuple-element.37, pred[512]{0:T(512)(128)(4,1)S(1)} %get-tuple-element.36, ...), kind=kLoop, calls=%fused_computation.89 | loop fusion | flops 16896 | bytes 21124 | tf_op jit(solution)/shard_map/jit(_take)/gather | solution.py:30
  145.7 1.0 slice.68
  146.7 0.9 copy.23
  147.5 0.2 broadcast.454
  147.7 29.9 %scatter_fusion = bf16[2,640,128]{2,0,1:T(2,128)(2,1)S(1)} fusion(bf16[2,640,128]{2,0,1:T(2,128)(2,1)S(1)} %broadcast.454, s32[512]{0:T(512)S(1)} %bitcast.86, bf16[512,2,128]{2,1,0:T(2,128)(2,1)} %bitcast.78), kind=kCustom, calls=%fused_computation.1 | custom fusion | bytes 788480 | tf_op jit(solution)/shard_map/scatter | solution.py:117
  177.6 0.8 copy.22
  178.3 48.1 %reduce-scatter.2.cloned.1.call-done = bf16[32,4096]{1,0:T(8,128)(2,1)} async-done(((bf16[512,4096]{1,0:T(8,128)(2,1)}), bf16[32,4096]{1,0:T(8,128)(2,1)}) %reduce-scatter.2.cloned.1.call-update) | async-done | bytes 262160 | tf_op jit(solution)/shard_map/reduce_scatter | solution.py:106
  (22 shorter events, 0.1 us)
Async XLA Ops:
  7.2 91.6 %copy-start = (bf16[4096,384]{1,0:T(8,128)(2,1)S(1)}, bf16[4096,384]{1,0:T(8,128)(2,1)}, u32[]{:S(2)}) copy-start(bf16[4096,384]{1,0:T(8,128)(2,1)} %param.11) | copy-start | bytes 9437188
  7.2 91.6 %all-gather.2.cloned.1.call-start = ((), (), s32[]{:S(2)}) async-start(), calls=%async_computation.1 | async-start | bytes 4456448 | tf_op jit(solution)/shard_map/all_gather | solution.py:89
  12.2 214.2 %reduce-scatter.2.cloned.1.call-start = ((), (), s32[]{:S(2)}) async-start(), calls=%async_computation.2 | async-start | bytes 4456448 | tf_op jit(solution)/shard_map/reduce_scatter | solution.py:106
  17.7 5.3 %copy-start.6 = (s32[512]{0:T(512)}, s32[512]{0:T(512)S(1)}, u32[]{:S(2)}) copy-start(s32[512]{0:T(512)S(1)} %get-tuple-element.50) | copy-start | bytes 6148
  102.8 6.4 %copy-start.3 = (bf16[512,384]{0,1:T(8,128)(2,1)}, bf16[512,384]{0,1:T(8,128)(2,1)S(1)}, u32[]{:S(2)}) copy-start(bf16[512,384]{0,1:T(8,128)(2,1)S(1)} %convolution_convert_fusion.1) | copy-start | bytes 1179652
  109.3 1.5 copy-start.1
  109.3 2.0 copy-start.7
  109.3 2.0 copy-start.4
  109.3 2.0 copy-start.5
  117.7 0.7 copy-start.2
Sparse Core Ops, SparseCore 0:
  12.3 86.4 all-gather.1
  117.8 108.5 reduce-scatter.1
where the time goes:
time: 236 us; the launch traced here: 233 us
  waiting for transfers between devices  124 us (53%)
  local copies, waits for them, and re-layouts  43.7 us (19%)
  other arithmetic  38.6 us (16%)
  between operations  14.3 us (6%)
  matrix products  12.7 us (5%)
    all_gather x1, waiting for transfers between devices, body(): lax.all_gather(normed, 'tp', axis=0, tiled=True)  75.8 us
    reduce_scatter x1, waiting for transfers between devices, body(): lax.psum_scatter(jnp.dot(contexts, out_weight, preferred_element_type=jnp...  48.1 us
    scatter x1, local copies, waits for them, and re-layouts, body(): fresh_pages = jnp.zeros((2, head_dev, fresh_total * page_len, head_size),...  29.9 us
    gather x3, other arithmetic, token_layout(): target = jnp.take(fresh_order, page_slot) * page_len + in_prompt % page_len  25.2 us
    dot_general x1, matrix products, body(): jnp.dot(contexts, out_weight, preferred_element_type=jnp.float32)  6.32 us
  transfers between devices with their start and end apart: 2, of which 2 were waited for; matrix products, arithmetic and copies ran while one was open for 30% of the time, Pallas kernels for 0%

commit v1 on v0

--- a/solution.py
+++ b/solution.py
@@ -4,6 +4,13 @@
 from jax.sharding import PartitionSpec as P
 
 MODEL_HEADS = 32
+
+
+def exchange_gather(array, axis, dim):
+    peers = lax.axis_size(axis)
+    blocks = jnp.stack([array for _ in range(peers)])
+    blocks = lax.all_to_all(blocks, axis, split_axis=0, concat_axis=0)
+    return jnp.concatenate(blocks, axis=dim)
 
 
 def layer_norm(values, gain):
@@ -86,9 +93,7 @@
     first_head = lax.axis_index("tp") * head_dev
     normed = layer_norm(tokens, norm_gain)
     projected = jnp.dot(
-        lax.all_gather(normed, "tp", axis=0, tiled=True),
-        qkv_weight,
-        preferred_element_type=jnp.float32,
+        exchange_gather(normed, "tp", 0), qkv_weight, preferred_element_type=jnp.float32
     ).astype(jnp.bfloat16)
     tok_count = projected.shape[0]
     in_prompt, position, target, key_owner, key_pos = token_layout(

time: 236 us -> 273 us (1.16)
  waiting for transfers between devices: 124 us -> 145 us
  starting transfers between devices: 0.08 us -> 8.99 us
  local copies, waits for them, and re-layouts: 43.7 us -> 48.4 us
  other arithmetic: 38.6 us -> 41.4 us
    all_to_all x0 -> x1, waiting for transfers between devices: none -> 83.4 us  [exchange_gather(): blocks = lax.all_to_all(blocks, axis, split_axis=0, concat_axis=0)]
    all_gather x1 -> x0, waiting for transfers between devices: 75.8 us -> none  [body(): lax.all_gather(normed, 'tp', axis=0, tiled=True)]
    reduce_scatter x1, waiting for transfers between devices: 48.1 us -> 61.5 us  [body(): lax.psum_scatter(jnp.dot(contexts, out_weight, preferred_element_type=jnp...]
    all_to_all x0 -> x1, starting transfers between devices: none -> 8.95 us  [exchange_gather(): blocks = lax.all_to_all(blocks, axis, split_axis=0, concat_axis=0)]
  transfers between devices with their start and end apart: 2 -> 2, of which waited for: 2 -> 2; matrix products, arithmetic and copies ran while one was open for 30% -> 28% of each run, Pallas kernels for 0% -> 0%
where the time goes in v1:
time: 273 us; the launch traced here: 271 us
  waiting for transfers between devices  145 us (53%)
  local copies, waits for them, and re-layouts  48.4 us (18%)
  other arithmetic  41.4 us (15%)
  between operations  14.3 us (5%)
  matrix products  12.7 us (5%)
  starting transfers between devices  8.99 us (3%)
    all_to_all x1, waiting for transfers between devices, exchange_gather(): blocks = lax.all_to_all(blocks, axis, split_axis=0, concat_axis=0)  83.4 us
    reduce_scatter x1, waiting for transfers between devices, body(): lax.psum_scatter(jnp.dot(contexts, out_weight, preferred_element_type=jnp...  61.5 us
    scatter x1, local copies, waits for them, and re-layouts, body(): fresh_pages = jnp.zeros((2, head_dev, fresh_total * page_len, head_size),...  29.9 us
    gather x3, other arithmetic, token_layout(): target = jnp.take(fresh_order, page_slot) * page_len + in_prompt % page_len  25.3 us
    all_to_all x1, starting transfers between devices, exchange_gather(): blocks = lax.all_to_all(blocks, axis, split_axis=0, concat_axis=0)  8.95 us
    dot_general x1, matrix products, body(): jnp.dot(contexts, out_weight, preferred_element_type=jnp.float32)  6.31 us
  transfers between devices with their start and end apart: 2, of which 2 were waited for; matrix products, arithmetic and copies ran while one was open for 28% of the time, Pallas kernels for 0%

profile of v1, /device:TPU:8, one launch (start us, length us, event | category | flops | bytes accessed | tf_op | source)
XLA Modules:
  0.0 270.6 jit_solution(2698689334590110422)
XLA Ops:
  7.2 0.9 convert_element_type.37
  8.0 1.2 convert_reduce_fusion
  9.2 1.2 fusion.7
  10.4 1.1 fusion.9
  11.5 2.5 stack.2
  14.0 8.9 %all-to-all-start = ((bf16[16,32,4096]{2,1,0:T(8,128)(2,1)}), bf16[16,32,4096]{2,1,0:T(8,128)(2,1)}, u32[]{:S(2)}, u32[]{:S(2)}) async-start(bf16[16,32,4096]{2,1,0:T(8,128)(2,1)} %stack.2), calls=%async_computation | async-start | bytes 8388608 | tf_op jit(solution)/shard_map/all_to_all | solution.py:12
  23.0 0.1 convert_reduce_fusion.1
  23.2 0.2 reduce-window.26
  23.4 0.5 and_select_fusion.4
  23.9 1.3 reduce-window.27
  25.2 0.7 reduce-window.25
  25.9 1.2 compare_select_fusion.11
  27.1 0.5 iota.25
  27.6 1.3 scatter_custom_fusion
  28.9 1.2 bitcast_subtract_fusion.1
  30.1 0.7 convert_reduce_fusion.2
  30.9 0.6 subtract_multiply_fusion
  31.5 0.7 iota_add_fusion
  32.1 0.8 add.182
  33.0 0.7 broadcast_in_dim.16
  33.7 0.8 eq.29
  34.5 1.2 select_reduce_fusion
  35.7 0.6 pad_add_fusion
  36.3 1.0 compare_and_fusion
  37.3 1.1 broadcast_compare_fusion
  38.4 0.8 fusion.26
  39.2 83.4 %all-to-all-done = bf16[16,32,4096]{2,1,0:T(8,128)(2,1)} async-done(((bf16[16,32,4096]{2,1,0:T(8,128)(2,1)}), bf16[16,32,4096]{2,1,0:T(8,128)(2,1)}, u32[]{:S(2)}, u32[]{:S(2)}) %all-to-all-start) | async-done | bytes 4194336 | tf_op jit(solution)/shard_map/all_to_all | solution.py:12
  122.6 4.0 %convolution_convert_fusion.1 = bf16[512,384]{0,1:T(8,128)(2,1)S(1)} fusion(bf16[512,4096]{1,0:T(8,128)(2,1)} %bitcast.4, bf16[4096,384]{1,0:T(8,128)(2,1)S(1)} %copy-done), kind=kOutput, calls=%fused_computation.10 | convolution fusion | flops 1610809344 | bytes 7733248 | tf_op jit(solution)/shard_map/dot_general | solution.py:95
  126.6 0.8 slice_bitcast_fusion
  127.4 1.7 copy.19
  129.1 1.7 copy.20
  130.7 2.3 fusion.30
  133.1 1.5 copy-done.1
  134.6 0.5 fusion.2
  135.2 6.3 %convolution_convert_fusion = bf16[512,4096]{1,0:T(8,128)(2,1)} fusion(bf16[128,4096]{1,0:T(8,128)(2,1)} %param.12, f32[512,1280]{1,0:T(8,128)} %copy-done.1, f32[512]{0:T(512)S(1)} %fusion.2, f32[512]{0:T(512)} %copy-done.12, bf16[512,128]{1,0:T(8,128)(2,1)S(1)} %copy-done.6, bf16[768,128]{1,0:T(8,128)(2,1)S(1)} %bitcast.81), kind=kOutput, calls=%fused_computation.2 | convolution fusion | flops 709427200 | bytes 8196096 | tf_op jit(solution)/shard_map/dot_general | solution.py:112
  141.5 0.6 copy-done.2
  142.1 0.6 fusion.29
  142.8 0.7 fusion.28
  143.5 0.7 fusion.27
  144.2 4.4 %compare_select_fusion.2 = (s32[512,1]{0,1:T(1,128)S(1)}, s32[512,1]{0,1:T(1,128)S(1)}) fusion(s32[]{:T(128)} %bitcast.47, s32[]{:T(128)} %bitcast.48, s32[]{:T(128)} %bitcast.49, s32[]{:T(128)} %bitcast.50, s32[]{:T(128)} %bitcast.51, s32[]{:T(128)} %bitcast.53, s32[]{:T(128)} %bitcast.52, s32[512,1]{0,1:T(1,128)S(1)} %bitcast.86, s32[512,1]{0,1:T(1,128)S(1)} %bitcast.83), kind=kLoop, calls=%fused_computation.72 | loop fusion | flops 16384 | bytes 8220 | tf_op jit(solution)/shard_map/jit(_take)/gather | solution.py:37
  148.7 0.2 compare_reduce_fusion.32
  148.9 20.7 %select_select_fusion = s32[512]{0:T(512)S(1)} fusion(pred[512]{0:T(512)(128)(4,1)S(1)} %get-tuple-element.39, pred[512]{0:T(512)(128)(4,1)S(1)} %get-tuple-element.38, pred[512]{0:T(512)(128)(4,1)S(1)} %get-tuple-element.40, pred[512]{0:T(512)(128)(4,1)S(1)} %get-tuple-element.37, pred[512]{0:T(512)(128)(4,1)S(1)} %get-tuple-element.36, ...), kind=kLoop, calls=%fused_computation.89 | loop fusion | flops 16896 | bytes 21124 | tf_op jit(solution)/shard_map/jit(_take)/gather | solution.py:37
  169.6 1.0 slice.68
  170.6 0.9 copy.23
  171.4 0.2 broadcast.456
  171.6 29.9 %scatter_fusion = bf16[2,640,128]{2,0,1:T(2,128)(2,1)S(1)} fusion(bf16[2,640,128]{2,0,1:T(2,128)(2,1)S(1)} %broadcast.456, s32[512]{0:T(512)S(1)} %bitcast.85, bf16[512,2,128]{2,1,0:T(2,128)(2,1)} %bitcast.77), kind=kCustom, calls=%fused_computation.1 | custom fusion | bytes 788480 | tf_op jit(solution)/shard_map/scatter | solution.py:122
  201.5 0.8 copy.22
  202.3 61.5 %reduce-scatter.2.cloned.1.call-done = bf16[32,4096]{1,0:T(8,128)(2,1)} async-done(((bf16[512,4096]{1,0:T(8,128)(2,1)}), bf16[32,4096]{1,0:T(8,128)(2,1)}) %reduce-scatter.2.cloned.1.call-update) | async-done | bytes 262160 | tf_op jit(solution)/shard_map/reduce_scatter | solution.py:111
  (34 shorter events, 0.2 us)
Async XLA Ops:
  7.2 115.4 %copy-start = (bf16[4096,384]{1,0:T(8,128)(2,1)S(1)}, bf16[4096,384]{1,0:T(8,128)(2,1)}, u32[]{:S(2)}) copy-start(bf16[4096,384]{1,0:T(8,128)(2,1)} %param.11) | copy-start | bytes 9437188
  14.0 9.0 %copy-start.7 = (s32[512]{0:T(512)S(1)}, s32[512]{0:T(512)}, u32[]{:S(2)}) copy-start(s32[512]{0:T(512)} %param.13) | copy-start | bytes 6148
  14.0 11.2 %copy-start.13 = (s32[8]{0:T(128)S(1)}, s32[8]{0:T(128)}, u32[]{:S(2)}) copy-start(s32[8]{0:T(128)} %param.14) | copy-start | bytes 100
  14.0 24.4 %copy-start.4 = (bf16[2,1,48,16,128]{4,3,2,1,0:T(8,128)(2,1)S(1)}, bf16[2,1,48,16,128]{4,3,2,1,0:T(8,128)(2,1)}, u32[]{:S(2)}) copy-start(bf16[2,1,48,16,128]{4,3,2,1,0:T(8,128)(2,1)} %param.17) | copy-start | bytes 1179652
  14.0 108.5 %all-to-all-start = ((bf16[16,32,4096]{2,1,0:T(8,128)(2,1)}), bf16[16,32,4096]{2,1,0:T(8,128)(2,1)}, u32[]{:S(2)}, u32[]{:S(2)}) async-start(bf16[16,32,4096]{2,1,0:T(8,128)(2,1)} %stack.2), calls=%async_computation | async-start | bytes 8388608 | tf_op jit(solution)/shard_map/all_to_all | solution.py:12
  23.0 240.8 %reduce-scatter.2.cloned.1.call-start = ((), (), s32[]{:S(2)}) async-start(), calls=%async_computation.2 | async-start | bytes 4456448 | tf_op jit(solution)/shard_map/reduce_scatter | solution.py:111
  35.7 0.6 copy-start.10
  122.6 8.1 %copy-start.8 = (s32[1280]{0:T(1024)S(1)}, s32[1280]{0:T(1024)}, u32[]{:S(2)}) copy-start(s32[1280]{0:T(1024)} %pad_add_fusion) | copy-start | bytes 15364
  122.6 8.1 %copy-start.11 = (s32[512]{0:T(512)S(1)}, s32[512]{0:T(512)}, u32[]{:S(2)}) copy-start(s32[512]{0:T(512)} %copy-done.10) | copy-start | bytes 6148
  126.6 6.4 %copy-start.3 = (bf16[512,384]{0,1:T(8,128)(2,1)}, bf16[512,384]{0,1:T(8,128)(2,1)S(1)}, u32[]{:S(2)}) copy-start(bf16[512,384]{0,1:T(8,128)(2,1)S(1)} %convolution_convert_fusion.1) | copy-start | bytes 1179652
  133.1 1.5 copy-start.1
  133.1 2.1 copy-start.12
  133.1 2.0 copy-start.5
  133.1 2.0 copy-start.6
  141.5 0.7 copy-start.2
  141.5 2.8 %copy-start.9 = (s32[512]{0:T(512)S(1)}, s32[512]{0:T(512)}, u32[]{:S(2)}) copy-start(s32[512]{0:T(512)} %get-tuple-element.41) | copy-start | bytes 6148
Sparse Core Ops, SparseCore 0:
  141.6 122.1 reduce-scatter.1
